TPU v7x, 256 devices: a whole 4x4x8 slice. The times are simulated.
256 devices in a mesh: dp: 8 (over z), seq: 32 (over y, x, core).
Axes of the slice: x: 4, y: 4, z: 8, core: 2. Of those that a mesh axis runs over, the one named last changes fastest.
Arguments:
- queries: bfloat16 [256, 2, 128, 4096], P(('dp', 'seq')), parts along dimension 0, may hold values from -6 to 6
- key_heads: bfloat16 [256, 2, 128, 512], P(('dp', 'seq')), parts along dimension 0, may hold values from -6 to 6
- value_heads: bfloat16 [256, 2, 128, 512], P(('dp', 'seq')), parts along dimension 0, may hold values from -6 to 6
- out_grad: bfloat16 [256, 2, 128, 4096], P(('dp', 'seq')), parts along dimension 0, may hold values from -6 to 6
- doc_lengths: int32 [256], P('dp'), parts along dimension 0, may hold values from 1 to 384, 8192 in all
- block_reach: int32 [512], P('dp'), parts along dimension 0, may hold values from 0 to 3, as said below
Outputs:
- attended: bfloat16 [256, 2, 128, 4096], P(('dp', 'seq')), parts along dimension 0
- query_grad: bfloat16 [256, 2, 128, 4096], P(('dp', 'seq')), parts along dimension 0
- key_grad: bfloat16 [256, 2, 128, 512], P(('dp', 'seq')), parts along dimension 0
- value_grad: bfloat16 [256, 2, 128, 512], P(('dp', 'seq')), parts along dimension 0
There are 8 independent parts, one for each index of `dp`. A program takes and returns all parts, laid end to end along the dimension named above; each array names one. Nothing has to cross between parts.
Inputs may be any that keep to these rules, and one draw needn't show every extreme that they name: doc_lengths are positive, sum to 8192, and the longest is exactly 384. `block_reach`: the value 4 - 1 occurs in every draw.
All inputs are finite; a program needn't handle non-finite values.
Results may differ from a plain program's by a relative error of at most 0.025.
Values may be sent and summed in bfloat16 or wider, within the bound.
No kernel may reach another device: no remote copies, remote signals or barrier semaphores. Data moves between devices by JAX's collectives and lax.ppermute only.
A program may use at most 128 MiB of HBM per device.

v0:
```python
import jax
import jax.numpy as jnp
from jax import lax
from jax.sharding import PartitionSpec as P

HEAD_SIZE = 128
WIN = 4


masked_fill = -1e30


def shifted(shard, axis, by):
    length = lax.axis_size(axis)
    pairs = [(i, i + by) for i in range(length) if 0 <= i + by < length]
    return lax.ppermute(shard, axis, pairs)


def doc_index(positions, doc_ends):
    return jnp.sum((positions[:, None] >= doc_ends[None, :]).astype(jnp.int32), axis=1)


def attend(queries_blk, grads_blk, window, first_key, block_index, reach_now, doc_ends):
    block_rows = queries_blk.shape[0]
    key_rows = window.shape[0]
    kv_width = window.shape[1] // 2
    heads_kv = kv_width // HEAD_SIZE
    group_size = queries_blk.shape[1] // kv_width
    score_scale = HEAD_SIZE ** (-0.5)
    q_four = queries_blk.reshape(block_rows, heads_kv, group_size, HEAD_SIZE)
    g_four = grads_blk.reshape(block_rows, heads_kv, group_size, HEAD_SIZE)
    k_three = window[:, :kv_width].reshape(key_rows, heads_kv, HEAD_SIZE)
    v_three = window[:, kv_width:].reshape(key_rows, heads_kv, HEAD_SIZE)
    query_pos = block_index * block_rows + jnp.arange(block_rows, dtype=jnp.int32)
    key_pos = first_key + jnp.arange(key_rows, dtype=jnp.int32)
    allowed = (key_pos[None, :] <= query_pos[:, None]) & (key_pos[None, :] >= 0)
    allowed = allowed & (
        doc_index(key_pos, doc_ends)[None, :] == doc_index(query_pos, doc_ends)[:, None]
    )
    allowed = allowed & (key_pos[None, :] // block_rows >= block_index - reach_now)
    scores = (
        jnp.einsum("tkgd,skd->kgts", q_four, k_three, preferred_element_type=jnp.float32)
        * score_scale
    )
    masked = jnp.where(allowed, scores, masked_fill)
    row_max = jnp.max(masked, axis=-1, keepdims=True)
    row_sum = jnp.sum(jnp.exp(masked - row_max), axis=-1, keepdims=True)
    log_total = row_max + jnp.log(row_sum)
    weights = jnp.exp(masked - log_total)
    weights_low = weights.astype(jnp.bfloat16)
    attended = jnp.einsum(
        "kgts,skd->tkgd", weights_low, v_three, preferred_element_type=jnp.float32
    ).astype(jnp.bfloat16)
    row_delta = jnp.einsum("tkgd,tkgd->kgt", g_four, attended, preferred_element_type=jnp.float32)
    weight_grad = jnp.einsum("tkgd,skd->kgts", g_four, v_three, preferred_element_type=jnp.float32)
    score_grad = (weights * (weight_grad - row_delta[..., None]) * score_scale).astype(jnp.bfloat16)
    query_grad = jnp.einsum(
        "kgts,skd->tkgd", score_grad, k_three, preferred_element_type=jnp.float32
    ).astype(jnp.bfloat16)
    key_part = jnp.einsum("kgts,tkgd->skd", score_grad, q_four, preferred_element_type=jnp.float32)
    value_part = jnp.einsum(
        "kgts,tkgd->skd", weights_low, g_four, preferred_element_type=jnp.float32
    )
    partials = jnp.concatenate(
        [key_part.reshape(key_rows, kv_width), value_part.reshape(key_rows, kv_width)], axis=1
    )
    return (attended.reshape(block_rows, -1), query_grad.reshape(block_rows, -1), partials)


def window_hops(own_low, own_high, device_index, seq_devices):
    last_device = device_index == seq_devices - 1
    blocks_low = [own_low]
    blocks_high = [own_high]
    current_low, current_high = (own_low, own_high)
    for hop_index in range(WIN - 1):
        from_below = shifted(current_low, "seq", 1)
        from_above = shifted(current_high, "seq", -1)
        current_high = jnp.where(last_device, current_low, from_above)
        current_low = from_below
        blocks_low.insert(0, current_low)
        blocks_high.insert(0, current_high)
    return (jnp.concatenate(blocks_low, axis=0), jnp.concatenate(blocks_high, axis=0))


def return_hops(partial_low, partial_high, device_index, seq_devices, block_rows):
    last_device = device_index == seq_devices - 1
    total_low = partial_low[:block_rows]
    total_high = partial_high[:block_rows]
    for hop_index in range(1, WIN):
        from_above = shifted(total_low, "seq", -1)
        from_below = shifted(total_high, "seq", 1)
        from_above = jnp.where(last_device, total_high, from_above)
        total_low = from_above + partial_low[hop_index * block_rows : (hop_index + 1) * block_rows]
        total_high = (
            from_below + partial_high[hop_index * block_rows : (hop_index + 1) * block_rows]
        )
    return (total_low, total_high)


def shards(queries, key_heads, value_heads, out_grad, doc_lengths, block_reach):
    seq_devices = lax.axis_size("seq")
    device_index = lax.axis_index("seq")
    block_rows = queries.shape[2]
    kv_width = key_heads.shape[3]
    doc_ends = jnp.cumsum(doc_lengths)
    own_blocks = jnp.concatenate([key_heads[0], value_heads[0]], axis=-1)
    window_low, window_high = window_hops(own_blocks[0], own_blocks[1], device_index, seq_devices)
    block_high = 2 * seq_devices - 1 - device_index
    results = []
    for slot_index, block_index, window in (
        (0, device_index, window_low),
        (1, block_high, window_high),
    ):
        reach_now = lax.dynamic_index_in_dim(block_reach, block_index, keepdims=False)
        outcome = attend(
            queries[0, slot_index],
            out_grad[0, slot_index],
            window,
            (block_index - WIN + 1) * block_rows,
            block_index,
            reach_now,
            doc_ends,
        )
        results.append(outcome)
    total_low, total_high = return_hops(
        results[0][2], results[1][2], device_index, seq_devices, block_rows
    )
    attended = jnp.stack([results[0][0], results[1][0]], axis=0)[None]
    query_grad = jnp.stack([results[0][1], results[1][1]], axis=0)[None]
    gradients = jnp.stack([total_low, total_high], axis=0)[None]
    key_grad = gradients[..., :kv_width].astype(jnp.bfloat16)
    value_grad = gradients[..., kv_width:].astype(jnp.bfloat16)
    return (attended, query_grad, key_grad, value_grad)


def solution(mesh):
    in_specs = (
        P(("dp", "seq"), None, None, None),
        P(("dp", "seq"), None, None, None),
        P(("dp", "seq"), None, None, None),
        P(("dp", "seq"), None, None, None),
        P("dp"),
        P("dp"),
    )
    out_specs = (
        P(("dp", "seq"), None, None, None),
        P(("dp", "seq"), None, None, None),
        P(("dp", "seq"), None, None, None),
        P(("dp", "seq"), None, None, None),
    )
    return jax.shard_map(shards, mesh=mesh, in_specs=in_specs, out_specs=out_specs, check_vma=False)
```

profile of v0, /device:TPU:56, one launch (start us, length us, event | category | flops | bytes accessed | tf_op | source)
XLA Modules:
  0.0 140.9 jit_solution(17210883013855363814)
XLA Ops:
  0.7 1.1 copy.66
  2.9 4.3 %collective-permute-start.3 = (bf16[128,1024]{0,1:T(8,128)(2,1)S(1)}, bf16[128,1024]{0,1:T(8,128)(2,1)}, u32[]{:S(2)}, u32[]{:S(2)}) collective-permute-start(bf16[128,1024]{0,1:T(8,128)(2,1)S(1)} %fusion.29), channel_id=1, source_target_pairs={{1,0},{2,1},{3,2},{4,3},{5,4},{6,5},{7,6},{8,7},{9,8},{10,9},{11,1... | collective-permute-start | bytes 786440 | tf_op jit(solution)/shard_map/ppermute | solution.py:16
  7.3 2.7 %fusion.59 = (bf16[1,1,128,4096]{3,2,1,0:T(8,128)(2,1)S(1)}, bf16[1,1,128,4096]{3,2,1,0:T(8,128)(2,1)}) fusion(bf16[1,2,128,4096]{3,2,1,0:T(8,128)(2,1)} %param.6), kind=kLoop, calls=%fused_computation.112 | loop fusion | bytes 4194304 | tf_op jit(solution)/shard_map/slice | solution.py:116
  10.0 2.7 %fusion.58 = (bf16[1,1,128,4096]{3,2,1,0:T(8,128)(2,1)}, bf16[1,1,128,4096]{3,2,1,0:T(8,128)(2,1)S(1)}) fusion(bf16[1,2,128,4096]{3,2,1,0:T(8,128)(2,1)} %param.9), kind=kLoop, calls=%fused_computation.111 | loop fusion | bytes 4194304 | tf_op jit(solution)/shard_map/slice | solution.py:117
  15.0 3.2 %collective-permute-start.4 = (bf16[128,1024]{0,1:T(8,128)(2,1)S(1)}, bf16[128,1024]{0,1:T(8,128)(2,1)S(1)}, u32[]{:S(2)}, u32[]{:S(2)}) collective-permute-start(bf16[128,1024]{0,1:T(8,128)(2,1)S(1)} %get-tuple-element.22), channel_id=1, source_target_pairs={{1,0},{2,1},{3,2},{4,3},{5,4},{6,5},{7,6},{8,7},{9,8},{10,9},{11,1... | collective-permute-start | bytes 786440 | tf_op jit(solution)/shard_map/ppermute | solution.py:16
  18.2 1.9 %collective-permute-start = (bf16[128,1024]{0,1:T(8,128)(2,1)S(1)}, bf16[128,1024]{0,1:T(8,128)(2,1)}, u32[]{:S(2)}, u32[]{:S(2)}) collective-permute-start(bf16[128,1024]{0,1:T(8,128)(2,1)S(1)} %get-tuple-element.23), channel_id=1, source_target_pairs={{0,1},{1,2},{2,3},{3,4},{4,5},{5,6},{6,7},{7,8},{8,9},{9,10},{10,1... | collective-permute-start | bytes 786440 | tf_op jit(solution)/shard_map/ppermute | solution.py:16
  22.1 6.0 %collective-permute-done = bf16[128,1024]{0,1:T(8,128)(2,1)} collective-permute-done((bf16[128,1024]{0,1:T(8,128)(2,1)S(1)}, bf16[128,1024]{0,1:T(8,128)(2,1)}, u32[]{:S(2)}, u32[]{:S(2)}) %collective-permute-start) | collective-permute-done | bytes 262176 | tf_op jit(solution)/shard_map/ppermute | solution.py:16
  28.9 1.9 %collective-permute-start.5 = (bf16[128,1024]{0,1:T(8,128)(2,1)}, bf16[128,1024]{0,1:T(8,128)(2,1)}, u32[]{:S(2)}, u32[]{:S(2)}) collective-permute-start(bf16[128,1024]{0,1:T(8,128)(2,1)} %broadcast_select_fusion.1), channel_id=1, source_target_pairs={{1,0},{2,1},{3,2},{4,3},{5,4},{6,5},{7,6},{8,7},{9,8},{10,9},{11,1... | collective-permute-start | bytes 786440 | tf_op jit(solution)/shard_map/ppermute | solution.py:16
  30.8 2.4 %collective-permute-start.1 = (bf16[128,1024]{0,1:T(8,128)(2,1)}, bf16[128,1024]{0,1:T(8,128)(2,1)}, u32[]{:S(2)}, u32[]{:S(2)}) collective-permute-start(bf16[128,1024]{0,1:T(8,128)(2,1)} %collective-permute-done), channel_id=1, source_target_pairs={{0,1},{1,2},{2,3},{3,4},{4,5},{5,6},{6,7},{7,8},{8,9},{9,10},{10,1... | collective-permute-start | bytes 786440 | tf_op jit(solution)/shard_map/ppermute | solution.py:16
  33.9 1.6 %copy.142 = bf16[1,1,128,4096]{2,3,1,0:T(8,128)(2,1)S(1)} copy(bf16[1,1,128,4096]{3,2,1,0:T(8,128)(2,1)} %get-tuple-element.27) | data formatting | bytes 2097152
  35.5 2.3 %copy.143 = bf16[1,1,128,4096]{2,3,1,0:T(8,128)(2,1)} copy(bf16[1,1,128,4096]{3,2,1,0:T(8,128)(2,1)} %get-tuple-element.24) | data formatting | bytes 2097152
  37.8 1.3 copy.144
  41.9 1.1 pad_maximum_fusion.1
  43.1 1.4 %fusion.9 = (f32[4,8,128]{2,1,0:T(8,128)S(1)}, f32[4,512,128,8]{2,1,3,0:T(8,128)S(1)}) fusion(pred[128,512]{0,1:T(8,128)(4,1)S(1)} %get-tuple-element.44, bf16[512,4,128,1]{0,2,3,1:T(8,128)(2,1)S(1)} %bitcast.186, bf16[128,4,8,128]{0,3,2,1:T(8,128)(2,1)S(1)} %bitcast.174), kind=kOutput, calls=%fused_computation.17 | convolution fusion | flops 543158272 | bytes 10043392 | tf_op jit(solution)/shard_map/tkgd,skd->kgts/dot_general | solution.py:42
  44.6 1.8 %exponential_reduce_fusion = f32[4,8,128]{2,1,0:T(8,128)S(1)} fusion(f32[4,512,128,8]{2,1,3,0:T(8,128)S(1)} %get-tuple-element.37, f32[4,8,128]{2,1,0:T(8,128)S(1)} %get-tuple-element.36, pred[128,512]{0,1:T(8,128)(4,1)S(1)} %get-tuple-element.44), kind=kLoop, calls=%fused_computation.11 | loop fusion | flops 8384512 | bytes 8486912 | tf_op jit(solution)/shard_map/reduce_sum | solution.py:47
  46.4 3.3 %fusion.10 = (f32[4,8,128]{2,1,0:T(8,128)S(1)}, bf16[4,128,8,128]{3,1,2,0:T(8,128)(2,1)}) fusion(bf16[4,8,128,128]{2,3,1,0:T(8,128)(2,1)S(1)} %bitcast.198, bf16[512,4,128,1]{0,2,3,1:T(8,128)(2,1)S(1)} %bitcast.204, f32[4,512,128,8]{2,1,3,0:T(8,128)S(1)} %get-tuple-element.37, f32[4,8,128]{2,1,0:T(8,128)S(1)} %log_add_fusion, ...), kind=kOutput, calls=%fused_computation.33 | convolution fusion | flops 547876864 | bytes 11108352 | tf_op jit(solution)/shard_map/kgts,skd->tkgd/dot_general | solution.py:51
  49.7 2.1 %collective-permute-start.2 = (bf16[128,1024]{0,1:T(8,128)(2,1)}, bf16[128,1024]{0,1:T(8,128)(2,1)S(1)}, u32[]{:S(2)}, u32[]{:S(2)}) collective-permute-start(bf16[128,1024]{0,1:T(8,128)(2,1)} %collective-permute-done.1), channel_id=1, source_target_pairs={{0,1},{1,2},{2,3},{3,4},{4,5},{5,6},{6,7},{7,8},{8,9},{9,10},{10,1... | collective-permute-start | bytes 786440 | tf_op jit(solution)/shard_map/ppermute | solution.py:16
  51.8 3.2 %fusion.2 = bf16[4,8,128,512]{2,3,1,0:T(8,128)(2,1)S(1)} fusion(f32[4,512,128,8]{2,1,3,0:T(8,128)S(1)} %get-tuple-element.37, f32[4,8,128]{2,1,0:T(8,128)S(1)} %get-tuple-element.40, f32[4,8,128]{2,1,0:T(8,128)S(1)} %log_add_fusion, pred[128,512]{0,1:T(8,128)(4,1)S(1)} %get-tuple-element.44, bf16[512,4,128,1]{0,2,3,1:T(8,128)(2,1)S(1)} %bitcast.205, ...), kind=kOutput, calls=%fused_computation.3 | convolution fusion | flops 551550976 | bytes 14254080 | tf_op jit(solution)/shard_map/tkgd,skd->kgts/dot_general | solution.py:55
  55.0 4.7 %collective-permute-done.2 = bf16[128,1024]{0,1:T(8,128)(2,1)S(1)} collective-permute-done((bf16[128,1024]{0,1:T(8,128)(2,1)}, bf16[128,1024]{0,1:T(8,128)(2,1)S(1)}, u32[]{:S(2)}, u32[]{:S(2)}) %collective-permute-start.2) | collective-permute-done | bytes 262176 | tf_op jit(solution)/shard_map/ppermute | solution.py:16
  59.7 1.1 pad_maximum_fusion
  60.9 1.4 %fusion.8 = (f32[4,8,128]{2,1,0:T(8,128)S(1)}, f32[4,512,128,8]{2,1,3,0:T(8,128)S(1)}) fusion(pred[128,512]{0,1:T(8,128)(4,1)S(1)} %get-tuple-element.45, bf16[512,4,128,1]{0,2,3,1:T(8,128)(2,1)S(1)} %bitcast.188, bf16[128,4,8,128]{0,3,2,1:T(8,128)(2,1)S(1)} %bitcast.176), kind=kOutput, calls=%fused_computation.16 | convolution fusion | flops 543158272 | bytes 10043392 | tf_op jit(solution)/shard_map/tkgd,skd->kgts/dot_general | solution.py:42
  62.4 1.8 %exponential_reduce_fusion.1 = f32[4,8,128]{2,1,0:T(8,128)S(1)} fusion(f32[4,512,128,8]{2,1,3,0:T(8,128)S(1)} %get-tuple-element.39, f32[4,8,128]{2,1,0:T(8,128)S(1)} %get-tuple-element.38, pred[128,512]{0,1:T(8,128)(4,1)S(1)} %get-tuple-element.45), kind=kLoop, calls=%fused_computation.13 | loop fusion | flops 8384512 | bytes 8486912 | tf_op jit(solution)/shard_map/reduce_sum | solution.py:47
  64.2 3.2 %fusion.33 = f32[4,512,128,1]{1,2,3,0:T(8,128)} fusion(bf16[128,4,8,128]{0,3,2,1:T(8,128)(2,1)S(1)} %bitcast.201, f32[4,512,128,8]{2,1,3,0:T(8,128)S(1)} %get-tuple-element.39, f32[4,8,128]{2,1,0:T(8,128)S(1)} %log_add_fusion.1, pred[128,512]{0,1:T(8,128)(4,1)S(1)} %get-tuple-element.45), kind=kOutput, calls=%fused_computation.72 | convolution fusion | flops 545259520 | bytes 10567680 | tf_op jit(solution)/shard_map/kgts,tkgd->skd/dot_general | solution.py:61
  67.4 3.3 %fusion.11 = (f32[4,8,128]{2,1,0:T(8,128)S(1)}, bf16[4,128,8,128]{3,1,2,0:T(8,128)(2,1)}) fusion(bf16[4,8,128,128]{2,3,1,0:T(8,128)(2,1)S(1)} %bitcast.202, bf16[512,4,128,1]{0,2,3,1:T(8,128)(2,1)S(1)} %bitcast.206, f32[4,512,128,8]{2,1,3,0:T(8,128)S(1)} %get-tuple-element.39, f32[4,8,128]{2,1,0:T(8,128)S(1)} %log_add_fusion.1, ...), kind=kOutput, calls=%fused_computation.35 | convolution fusion | flops 547876864 | bytes 11108352 | tf_op jit(solution)/shard_map/kgts,skd->tkgd/dot_general | solution.py:51
  70.7 4.3 %fusion.5 = bf16[4,8,128,512]{2,3,1,0:T(8,128)(2,1)S(1)} fusion(f32[4,512,128,8]{2,1,3,0:T(8,128)S(1)} %get-tuple-element.39, f32[4,8,128]{2,1,0:T(8,128)S(1)} %get-tuple-element.42, f32[4,8,128]{2,1,0:T(8,128)S(1)} %log_add_fusion.1, pred[128,512]{0,1:T(8,128)(4,1)S(1)} %get-tuple-element.45, bf16[512,4,128,1]{0,2,3,1:T(8,128)(2,1)} %bitcast.207, ...), kind=kOutput, calls=%fused_computation.7 | convolution fusion | flops 551550976 | bytes 14254080 | tf_op jit(solution)/shard_map/tkgd,skd->kgts/dot_general | solution.py:55
  75.0 1.5 %fusion.65 = f32[4,512,128,1]{1,2,3,0:T(8,128)S(1)} fusion(bf16[4,8,128,512]{2,3,1,0:T(8,128)(2,1)S(1)} %fusion.5, bf16[128,4,8,128]{0,3,2,1:T(8,128)(2,1)S(1)} %bitcast.177), kind=kOutput, calls=%fused_computation.118 | convolution fusion | flops 536870912 | bytes 6291456 | tf_op jit(solution)/shard_map/kgts,tkgd->skd/dot_general | solution.py:60
  77.1 2.3 %collective-permute-start.8 = (f32[128,1024]{0,1:T(8,128)S(1)}, f32[128,1024]{0,1:T(8,128)S(1)}, u32[]{:S(2)}, u32[]{:S(2)}) collective-permute-start(f32[128,1024]{0,1:T(8,128)S(1)} %fusion.15), channel_id=1, source_target_pairs={{1,0},{2,1},{3,2},{4,3},{5,4},{6,5},{7,6},{8,7},{9,8},{10,9},{11,1... | collective-permute-start | bytes 1572872 | tf_op jit(solution)/shard_map/ppermute | solution.py:16
  79.4 2.2 %fusion.30 = f32[4,512,128,1]{1,2,3,0:T(8,128)S(1)} fusion(bf16[128,4,8,128]{0,3,2,1:T(8,128)(2,1)S(1)} %bitcast.200, f32[4,512,128,8]{2,1,3,0:T(8,128)S(1)} %get-tuple-element.37, f32[4,8,128]{2,1,0:T(8,128)S(1)} %log_add_fusion, pred[128,512]{0,1:T(8,128)(4,1)S(1)} %get-tuple-element.44), kind=kOutput, calls=%fused_computation.71 | convolution fusion | flops 545259520 | bytes 10567680 | tf_op jit(solution)/shard_map/kgts,tkgd->skd/dot_general | solution.py:61
  81.5 1.5 %fusion.64 = f32[4,512,128,1]{1,2,3,0:T(8,128)S(1)} fusion(bf16[4,8,128,512]{2,3,1,0:T(8,128)(2,1)S(1)} %fusion.2, bf16[128,4,8,128]{0,3,2,1:T(8,128)(2,1)S(1)} %bitcast.175), kind=kOutput, calls=%fused_computation.117 | convolution fusion | flops 536870912 | bytes 6291456 | tf_op jit(solution)/shard_map/kgts,tkgd->skd/dot_general | solution.py:60
  83.0 2.8 %collective-permute-done.8 = f32[128,1024]{0,1:T(8,128)S(1)} collective-permute-done((f32[128,1024]{0,1:T(8,128)S(1)}, f32[128,1024]{0,1:T(8,128)S(1)}, u32[]{:S(2)}, u32[]{:S(2)}) %collective-permute-start.8) | collective-permute-done | bytes 524320 | tf_op jit(solution)/shard_map/ppermute | solution.py:16
  85.9 5.9 %collective-permute-start.9 = (f32[128,1024]{0,1:T(8,128)S(1)}, f32[128,1024]{0,1:T(8,128)S(1)}, u32[]{:S(2)}, u32[]{:S(2)}) collective-permute-start(f32[128,1024]{0,1:T(8,128)S(1)} %get-tuple-element.20), channel_id=1, source_target_pairs={{1,0},{2,1},{3,2},{4,3},{5,4},{6,5},{7,6},{8,7},{9,8},{10,9},{11,1... | collective-permute-start | bytes 1572872 | tf_op jit(solution)/shard_map/ppermute | solution.py:16
  91.8 1.9 %collective-permute-start.6 = (f32[128,1024]{0,1:T(8,128)S(1)}, f32[128,1024]{0,1:T(8,128)S(1)}, u32[]{:S(2)}, u32[]{:S(2)}) collective-permute-start(f32[128,1024]{0,1:T(8,128)S(1)} %get-tuple-element.21), channel_id=1, source_target_pairs={{0,1},{1,2},{2,3},{3,4},{4,5},{5,6},{6,7},{7,8},{8,9},{9,10},{10,1... | collective-permute-start | bytes 1572872 | tf_op jit(solution)/shard_map/ppermute | solution.py:16
  93.8 4.7 %collective-permute-done.9 = f32[128,1024]{0,1:T(8,128)S(1)} collective-permute-done((f32[128,1024]{0,1:T(8,128)S(1)}, f32[128,1024]{0,1:T(8,128)S(1)}, u32[]{:S(2)}, u32[]{:S(2)}) %collective-permute-start.9) | collective-permute-done | bytes 524320 | tf_op jit(solution)/shard_map/ppermute | solution.py:16
  98.5 5.9 %collective-permute-done.6 = f32[128,1024]{0,1:T(8,128)S(1)} collective-permute-done((f32[128,1024]{0,1:T(8,128)S(1)}, f32[128,1024]{0,1:T(8,128)S(1)}, u32[]{:S(2)}, u32[]{:S(2)}) %collective-permute-start.6) | collective-permute-done | bytes 524320 | tf_op jit(solution)/shard_map/ppermute | solution.py:16
  105.5 1.9 %collective-permute-start.10 = (f32[128,1024]{0,1:T(8,128)}, f32[128,1024]{0,1:T(8,128)}, u32[]{:S(2)}, u32[]{:S(2)}) collective-permute-start(f32[128,1024]{0,1:T(8,128)} %get-tuple-element.18), channel_id=1, source_target_pairs={{1,0},{2,1},{3,2},{4,3},{5,4},{6,5},{7,6},{8,7},{9,8},{10,9},{11,1... | collective-permute-start | bytes 1572872 | tf_op jit(solution)/shard_map/ppermute | solution.py:16
  107.5 2.4 %collective-permute-start.7 = (f32[128,1024]{0,1:T(8,128)}, f32[128,1024]{0,1:T(8,128)}, u32[]{:S(2)}, u32[]{:S(2)}) collective-permute-start(f32[128,1024]{0,1:T(8,128)} %get-tuple-element.19), channel_id=1, source_target_pairs={{0,1},{1,2},{2,3},{3,4},{4,5},{5,6},{6,7},{7,8},{8,9},{9,10},{10,1... | collective-permute-start | bytes 1572872 | tf_op jit(solution)/shard_map/ppermute | solution.py:16
  109.9 1.7 %convolution_convert_fusion = bf16[4,128,8,128]{3,1,2,0:T(8,128)(2,1)} fusion(bf16[512,4,128,1]{0,2,3,1:T(8,128)(2,1)S(1)} %bitcast.187, bf16[4,8,128,512]{2,3,1,0:T(8,128)(2,1)S(1)} %fusion.2), kind=kOutput, calls=%fused_computation.36 | convolution fusion | flops 537395200 | bytes 5767168 | tf_op jit(solution)/shard_map/kgts,skd->tkgd/dot_general | solution.py:57
  111.6 2.4 %copy.88 = bf16[1,128,4096]{2,1,0:T(8,128)(2,1)} copy(bf16[1,128,4096]{1,2,0:T(8,128)(2,1)} %bitcast.190) | data formatting | bytes 2097152 | tf_op jit(solution)/shard_map/stack;reshape | solution.py:129
  114.0 2.3 %copy.78 = bf16[1,128,4096]{2,1,0:T(8,128)(2,1)} copy(bf16[1,128,4096]{1,2,0:T(8,128)(2,1)} %bitcast.196) | data formatting | bytes 2097152 | tf_op jit(solution)/shard_map/stack;reshape | solution.py:128
  116.4 4.1 %convolution_convert_fusion.1 = bf16[4,128,8,128]{3,1,2,0:T(8,128)(2,1)} fusion(bf16[512,4,128,1]{0,2,3,1:T(8,128)(2,1)} %bitcast.189, bf16[4,8,128,512]{2,3,1,0:T(8,128)(2,1)} %copy-done), kind=kOutput, calls=%fused_computation.37 | convolution fusion | flops 537395200 | bytes 5767168 | tf_op jit(solution)/shard_map/kgts,skd->tkgd/dot_general | solution.py:57
  120.4 2.3 %copy.87 = bf16[1,128,4096]{2,1,0:T(8,128)(2,1)} copy(bf16[1,128,4096]{1,2,0:T(8,128)(2,1)} %bitcast.191) | data formatting | bytes 2097152 | tf_op jit(solution)/shard_map/stack;reshape | solution.py:129
  122.7 2.2 %fusion.26 = (bf16[1,128,1024]{1,2,0:T(8,128)(2,1)S(1)}, f32[128,1024]{0,1:T(8,128)}) fusion(f32[512,512]{0,1:T(8,128)S(1)} %bitcast.181, f32[512,512]{0,1:T(8,128)S(1)} %bitcast.169, f32[128,1024]{0,1:T(8,128)} %collective-permute-done.10, pred[]{:T(512)S(6)} %eq.33, f32[128,1024]{0,1:T(8,128)} %collective-permute-done.7, f32[512,512]{0,1:T(8,128)} %bitcast.184, ...), kind=kLoop, calls=%fused_computation.59 | loop fusion | flops 786432 | bytes 6029313 | tf_op jit(solution)/shard_map/stack | solution.py:130
  124.9 2.0 %collective-permute-start.11 = (f32[128,1024]{0,1:T(8,128)}, f32[128,1024]{0,1:T(8,128)}, u32[]{:S(2)}, u32[]{:S(2)}) collective-permute-start(f32[128,1024]{0,1:T(8,128)} %get-tuple-element.17), channel_id=1, source_target_pairs={{0,1},{1,2},{2,3},{3,4},{4,5},{5,6},{6,7},{7,8},{8,9},{9,10},{10,1... | collective-permute-start | bytes 1572872 | tf_op jit(solution)/shard_map/ppermute | solution.py:16
  127.0 3.1 %maximum_bitcast_fusion.1 = bf16[1,2,128,4096]{3,2,1,0:T(8,128)(2,1)} fusion(bf16[1,128,4096]{2,1,0:T(8,128)(2,1)} %copy.88, bf16[1,128,4096]{2,1,0:T(8,128)(2,1)} %copy.87), kind=kLoop, calls=%fused_computation.31 | loop fusion | flops 1048576 | bytes 4194304 | tf_op jit(solution)/shard_map/broadcast_in_dim | solution.py:129
  130.0 1.5 %copy.77 = bf16[1,128,4096]{2,1,0:T(8,128)(2,1)S(1)} copy(bf16[1,128,4096]{1,2,0:T(8,128)(2,1)} %bitcast.197) | data formatting | bytes 2097152 | tf_op jit(solution)/shard_map/stack;reshape | solution.py:128
  131.5 2.7 %maximum_bitcast_fusion = bf16[1,2,128,4096]{3,2,1,0:T(8,128)(2,1)} fusion(bf16[1,128,4096]{2,1,0:T(8,128)(2,1)} %copy.78, bf16[1,128,4096]{2,1,0:T(8,128)(2,1)S(1)} %copy.77), kind=kLoop, calls=%fused_computation.30 | loop fusion | flops 1048576 | bytes 4194304 | tf_op jit(solution)/shard_map/broadcast_in_dim | solution.py:128
  134.2 3.7 %collective-permute-done.11 = f32[128,1024]{0,1:T(8,128)} collective-permute-done((f32[128,1024]{0,1:T(8,128)}, f32[128,1024]{0,1:T(8,128)}, u32[]{:S(2)}, u32[]{:S(2)}) %collective-permute-start.11) | collective-permute-done | bytes 524320 | tf_op jit(solution)/shard_map/ppermute | solution.py:16
  138.0 1.1 fusion.24
  (72 shorter events, 12.1 us)
Async XLA Ops:
  0.6 12.1 %copy-start.15 = (s32[64]{0:T(128)S(1)}, s32[64]{0:T(128)}, u32[]{:S(2)}) copy-start(s32[64]{0:T(128)} %param.11) | copy-start | bytes 772
  0.6 20.2 %copy-start.16 = (s32[32]{0:T(128)S(1)}, s32[32]{0:T(128)}, u32[]{:S(2)}) copy-start(s32[32]{0:T(128)} %param.10) | copy-start | bytes 388
  2.9 11.0 %collective-permute-start.3 = (bf16[128,1024]{0,1:T(8,128)(2,1)S(1)}, bf16[128,1024]{0,1:T(8,128)(2,1)}, u32[]{:S(2)}, u32[]{:S(2)}) collective-permute-start(bf16[128,1024]{0,1:T(8,128)(2,1)S(1)} %fusion.29), channel_id=1, source_target_pairs={{1,0},{2,1},{3,2},{4,3},{5,4},{6,5},{7,6},{8,7},{9,8},{10,9},{11,1... | collective-permute-start | bytes 786440 | tf_op jit(solution)/shard_map/ppermute | solution.py:16
  15.0 18.2 %copy-start.11 = (bf16[128,1024]{0,1:T(8,128)(2,1)}, bf16[128,1024]{0,1:T(8,128)(2,1)S(1)}, u32[]{:S(2)}) copy-start(bf16[128,1024]{0,1:T(8,128)(2,1)S(1)} %get-tuple-element.23) | copy-start | bytes 786436
  15.0 18.2 %copy-start.13 = (bf16[128,1024]{0,1:T(8,128)(2,1)}, bf16[128,1024]{0,1:T(8,128)(2,1)S(1)}, u32[]{:S(2)}) copy-start(bf16[128,1024]{0,1:T(8,128)(2,1)S(1)} %get-tuple-element.22) | copy-start | bytes 786436
  15.0 7.0 %collective-permute-start.4 = (bf16[128,1024]{0,1:T(8,128)(2,1)S(1)}, bf16[128,1024]{0,1:T(8,128)(2,1)S(1)}, u32[]{:S(2)}, u32[]{:S(2)}) collective-permute-start(bf16[128,1024]{0,1:T(8,128)(2,1)S(1)} %get-tuple-element.22), channel_id=1, source_target_pairs={{1,0},{2,1},{3,2},{4,3},{5,4},{6,5},{7,6},{8,7},{9,8},{10,9},{11,1... | collective-permute-start | bytes 786440 | tf_op jit(solution)/shard_map/ppermute | solution.py:16
  18.2 9.9 %collective-permute-start = (bf16[128,1024]{0,1:T(8,128)(2,1)S(1)}, bf16[128,1024]{0,1:T(8,128)(2,1)}, u32[]{:S(2)}, u32[]{:S(2)}) collective-permute-start(bf16[128,1024]{0,1:T(8,128)(2,1)S(1)} %get-tuple-element.23), channel_id=1, source_target_pairs={{0,1},{1,2},{2,3},{3,4},{4,5},{5,6},{6,7},{7,8},{8,9},{9,10},{10,1... | collective-permute-start | bytes 786440 | tf_op jit(solution)/shard_map/ppermute | solution.py:16
  28.9 11.0 %collective-permute-start.5 = (bf16[128,1024]{0,1:T(8,128)(2,1)}, bf16[128,1024]{0,1:T(8,128)(2,1)}, u32[]{:S(2)}, u32[]{:S(2)}) collective-permute-start(bf16[128,1024]{0,1:T(8,128)(2,1)} %broadcast_select_fusion.1), channel_id=1, source_target_pairs={{1,0},{2,1},{3,2},{4,3},{5,4},{6,5},{7,6},{8,7},{9,8},{10,9},{11,1... | collective-permute-start | bytes 786440 | tf_op jit(solution)/shard_map/ppermute | solution.py:16
  30.8 10.1 %collective-permute-start.1 = (bf16[128,1024]{0,1:T(8,128)(2,1)}, bf16[128,1024]{0,1:T(8,128)(2,1)}, u32[]{:S(2)}, u32[]{:S(2)}) collective-permute-start(bf16[128,1024]{0,1:T(8,128)(2,1)} %collective-permute-done), channel_id=1, source_target_pairs={{0,1},{1,2},{2,3},{3,4},{4,5},{5,6},{6,7},{7,8},{8,9},{9,10},{10,1... | collective-permute-start | bytes 786440 | tf_op jit(solution)/shard_map/ppermute | solution.py:16
  43.1 3.3 %copy-start.5 = (bf16[512,512]{0,1:T(8,128)(2,1)}, bf16[512,512]{0,1:T(8,128)(2,1)S(1)}, u32[]{:S(2)}) copy-start(bf16[512,512]{0,1:T(8,128)(2,1)S(1)} %get-tuple-element.30) | copy-start | bytes 1572868
  43.1 3.3 %copy-start.8 = (bf16[1,1,128,4096]{2,3,1,0:T(8,128)(2,1)S(1)}, bf16[1,1,128,4096]{2,3,1,0:T(8,128)(2,1)}, u32[]{:S(2)}) copy-start(bf16[1,1,128,4096]{2,3,1,0:T(8,128)(2,1)} %copy.144) | copy-start | bytes 3145732
  49.7 10.0 %collective-permute-start.2 = (bf16[128,1024]{0,1:T(8,128)(2,1)}, bf16[128,1024]{0,1:T(8,128)(2,1)S(1)}, u32[]{:S(2)}, u32[]{:S(2)}) collective-permute-start(bf16[128,1024]{0,1:T(8,128)(2,1)} %collective-permute-done.1), channel_id=1, source_target_pairs={{0,1},{1,2},{2,3},{3,4},{4,5},{5,6},{6,7},{7,8},{8,9},{9,10},{10,1... | collective-permute-start | bytes 786440 | tf_op jit(solution)/shard_map/ppermute | solution.py:16
  51.8 7.9 %copy-start.12 = (bf16[128,1024]{0,1:T(8,128)(2,1)S(1)}, bf16[128,1024]{0,1:T(8,128)(2,1)}, u32[]{:S(2)}) copy-start(bf16[128,1024]{0,1:T(8,128)(2,1)} %copy-done.11) | copy-start | bytes 786436
  60.9 3.3 %copy-start.7 = (bf16[512,512]{0,1:T(8,128)(2,1)}, bf16[512,512]{0,1:T(8,128)(2,1)S(1)}, u32[]{:S(2)}) copy-start(bf16[512,512]{0,1:T(8,128)(2,1)S(1)} %get-tuple-element.28) | copy-start | bytes 1572868
  60.9 6.5 %copy-start.14 = (bf16[512,512]{0,1:T(8,128)(2,1)}, bf16[512,512]{0,1:T(8,128)(2,1)S(1)}, u32[]{:S(2)}) copy-start(bf16[512,512]{0,1:T(8,128)(2,1)S(1)} %get-tuple-element.29) | copy-start | bytes 1572868
  60.9 3.3 %copy-start.10 = (bf16[1,1,128,4096]{2,3,1,0:T(8,128)(2,1)S(1)}, bf16[1,1,128,4096]{2,3,1,0:T(8,128)(2,1)}, u32[]{:S(2)}) copy-start(bf16[1,1,128,4096]{2,3,1,0:T(8,128)(2,1)} %copy.143) | copy-start | bytes 3145732
  75.0 6.5 %copy-start = (bf16[4,8,128,512]{2,3,1,0:T(8,128)(2,1)}, bf16[4,8,128,512]{2,3,1,0:T(8,128)(2,1)S(1)}, u32[]{:S(2)}) copy-start(bf16[4,8,128,512]{2,3,1,0:T(8,128)(2,1)S(1)} %fusion.5) | copy-start | bytes 12582916
  75.0 2.0 %copy-start.1 = (f32[4,512,128,1]{1,2,3,0:T(8,128)S(1)}, f32[4,512,128,1]{1,2,3,0:T(8,128)}, u32[]{:S(2)}) copy-start(f32[4,512,128,1]{1,2,3,0:T(8,128)} %fusion.33) | copy-start | bytes 3145732
  75.0 4.4 %copy-start.9 = (bf16[1,1,128,4096]{2,3,1,0:T(8,128)(2,1)S(1)}, bf16[1,1,128,4096]{2,3,1,0:T(8,128)(2,1)}, u32[]{:S(2)}) copy-start(bf16[1,1,128,4096]{2,3,1,0:T(8,128)(2,1)} %copy.144) | copy-start | bytes 3145732
  77.1 8.7 %collective-permute-start.8 = (f32[128,1024]{0,1:T(8,128)S(1)}, f32[128,1024]{0,1:T(8,128)S(1)}, u32[]{:S(2)}, u32[]{:S(2)}) collective-permute-start(f32[128,1024]{0,1:T(8,128)S(1)} %fusion.15), channel_id=1, source_target_pairs={{1,0},{2,1},{3,2},{4,3},{5,4},{6,5},{7,6},{8,7},{9,8},{10,9},{11,1... | collective-permute-start | bytes 1572872 | tf_op jit(solution)/shard_map/ppermute | solution.py:16
  81.5 24.0 %copy-start.3 = (f32[4,512,128,1]{1,2,3,0:T(8,128)}, f32[4,512,128,1]{1,2,3,0:T(8,128)S(1)}, u32[]{:S(2)}) copy-start(f32[4,512,128,1]{1,2,3,0:T(8,128)S(1)} %fusion.30) | copy-start | bytes 3145732
  83.0 26.9 %copy-start.6 = (bf16[512,512]{0,1:T(8,128)(2,1)S(1)}, bf16[512,512]{0,1:T(8,128)(2,1)}, u32[]{:S(2)}) copy-start(bf16[512,512]{0,1:T(8,128)(2,1)} %copy-done.5) | copy-start | bytes 1572868
  85.9 12.6 %collective-permute-start.9 = (f32[128,1024]{0,1:T(8,128)S(1)}, f32[128,1024]{0,1:T(8,128)S(1)}, u32[]{:S(2)}, u32[]{:S(2)}) collective-permute-start(f32[128,1024]{0,1:T(8,128)S(1)} %get-tuple-element.20), channel_id=1, source_target_pairs={{1,0},{2,1},{3,2},{4,3},{5,4},{6,5},{7,6},{8,7},{9,8},{10,9},{11,1... | collective-permute-start | bytes 1572872 | tf_op jit(solution)/shard_map/ppermute | solution.py:16
  91.8 12.6 %collective-permute-start.6 = (f32[128,1024]{0,1:T(8,128)S(1)}, f32[128,1024]{0,1:T(8,128)S(1)}, u32[]{:S(2)}, u32[]{:S(2)}) collective-permute-start(f32[128,1024]{0,1:T(8,128)S(1)} %get-tuple-element.21), channel_id=1, source_target_pairs={{0,1},{1,2},{2,3},{3,4},{4,5},{5,6},{6,7},{7,8},{8,9},{9,10},{10,1... | collective-permute-start | bytes 1572872 | tf_op jit(solution)/shard_map/ppermute | solution.py:16
  105.5 17.2 %collective-permute-start.10 = (f32[128,1024]{0,1:T(8,128)}, f32[128,1024]{0,1:T(8,128)}, u32[]{:S(2)}, u32[]{:S(2)}) collective-permute-start(f32[128,1024]{0,1:T(8,128)} %get-tuple-element.18), channel_id=1, source_target_pairs={{1,0},{2,1},{3,2},{4,3},{5,4},{6,5},{7,6},{8,7},{9,8},{10,9},{11,1... | collective-permute-start | bytes 1572872 | tf_op jit(solution)/shard_map/ppermute | solution.py:16
  107.5 15.2 %collective-permute-start.7 = (f32[128,1024]{0,1:T(8,128)}, f32[128,1024]{0,1:T(8,128)}, u32[]{:S(2)}, u32[]{:S(2)}) collective-permute-start(f32[128,1024]{0,1:T(8,128)} %get-tuple-element.19), channel_id=1, source_target_pairs={{0,1},{1,2},{2,3},{3,4},{4,5},{5,6},{6,7},{7,8},{8,9},{9,10},{10,1... | collective-permute-start | bytes 1572872 | tf_op jit(solution)/shard_map/ppermute | solution.py:16
  111.6 11.1 %copy-start.2 = (f32[4,512,128,1]{1,2,3,0:T(8,128)S(1)}, f32[4,512,128,1]{1,2,3,0:T(8,128)}, u32[]{:S(2)}) copy-start(f32[4,512,128,1]{1,2,3,0:T(8,128)} %fusion.33) | copy-start | bytes 3145732
  124.9 13.1 %copy-start.4 = (f32[4,512,128,1]{1,2,3,0:T(8,128)S(1)}, f32[4,512,128,1]{1,2,3,0:T(8,128)}, u32[]{:S(2)}) copy-start(f32[4,512,128,1]{1,2,3,0:T(8,128)} %copy-done.3) | copy-start | bytes 3145732
  124.9 13.0 %collective-permute-start.11 = (f32[128,1024]{0,1:T(8,128)}, f32[128,1024]{0,1:T(8,128)}, u32[]{:S(2)}, u32[]{:S(2)}) collective-permute-start(f32[128,1024]{0,1:T(8,128)} %get-tuple-element.17), channel_id=1, source_target_pairs={{0,1},{1,2},{2,3},{3,4},{4,5},{5,6},{6,7},{7,8},{8,9},{9,10},{10,1... | collective-permute-start | bytes 1572872 | tf_op jit(solution)/shard_map/ppermute | solution.py:16
where the time goes:
time: 142 us; the launch traced here: 141 us
  starting transfers between devices  32.3 us (23%)
  matrix products  31 us (22%)
  waiting for transfers between devices  29.8 us (21%)
  local copies, waits for them, and re-layouts  25.1 us (18%)
  other arithmetic  20.3 us (14%)
  between operations  2.51 us (2%)
    ppermute x12, starting transfers between devices, shifted(): return lax.ppermute(shard, axis, pairs)  32.3 us
    ppermute x12, waiting for transfers between devices, shifted(): return lax.ppermute(shard, axis, pairs)  29.8 us
    unnamed x42, local copies, waits for them, and re-layouts  10.4 us
    dot_general x2, matrix products, attend(): jnp.einsum('tkgd,skd->kgts', g_four, v_three, preferred_element_type=jnp....  7.49 us
    dot_general x2, matrix products, attend(): jnp.einsum('kgts,skd->tkgd', weights_low, v_three, preferred_element_type...  6.55 us
    dot_general x2, matrix products, attend(): jnp.einsum('kgts,skd->tkgd', score_grad, k_three, preferred_element_type=...  5.82 us
    dot_general x2, matrix products, attend(): jnp.einsum('kgts,tkgd->skd', weights_low, g_four, preferred_element_type=...  5.34 us
    another operation x2, local copies, waits for them, and re-layouts, shards(): query_grad = jnp.stack([results[0][1], results[1][1]], axis=0)[None]  4.68 us
  transfers between devices with their start and end apart: 12, of which 8 were waited for; matrix products, arithmetic and copies ran while one was open for 28% of the time, Pallas kernels for 0%

commit v1 on v0

v1 whole, which is shorter than its diff:
```python
import jax
import jax.numpy as jnp
from jax import lax
from jax.experimental import pallas as pl
from jax.experimental.pallas import tpu as pltpu
from jax.sharding import PartitionSpec as P

HEAD = 128
WIN = 4
LOG2E = 1.4426950408889634
MASKED = -1e30
NT = (((1,), (1,)), ((), ()))
TN = (((0,), (0,)), ((), ()))


def row_bias(info_ref, lens_ref, reach_ref, edge, rows):
    block = info_ref[2 + edge]
    reach = reach_ref[block]
    t = block * rows + lax.broadcasted_iota(jnp.int32, (rows, HEAD), 0)
    first = jnp.maximum((block - reach) * rows, 0)
    lo = jnp.zeros((rows, HEAD), jnp.int32) + first

    def one_doc(i, carry):
        lo, end = carry
        end = end + lens_ref[i]
        return jnp.where(end <= t, jnp.maximum(lo, end), lo), end

    lo, _ = lax.fori_loop(0, lens_ref.shape[0], one_doc, (lo, jnp.int32(0)), unroll=True)
    parts = []
    for w in range(WIN):
        s = (block - (WIN - 1) + w) * rows + lax.broadcasted_iota(jnp.int32, (rows, rows), 1)
        ok = (s <= t) & (s >= lo)
        parts.append(jnp.where(ok, 0.0, MASKED).astype(jnp.float32))
    return jnp.concatenate(parts, axis=1)


def attend_kernel(edge, aliased, info_ref, lens_ref, reach_ref, q_ref, g_ref, *refs):
    if aliased:
        refs = refs[:8] + refs[10:]
    (k3, v3, k2, v2, k1, v1, k0, v0,
     att_ref, dq_ref, far_ref, near_ref, bias_ref, p_all, ds_all, qs_all, gs_all) = refs
    rows = q_ref.shape[2]
    heads = q_ref.shape[3] // HEAD
    scale = HEAD ** -0.5
    c2 = scale * LOG2E

    @pl.when(pl.program_id(0) == 0)
    def _():
        bias_ref[...] = row_bias(info_ref, lens_ref, reach_ref, edge, rows)

    flat = lambda r: r[...].reshape(rows, HEAD)
    keys = jnp.concatenate([flat(k3), flat(k2), flat(k1), flat(k0)], axis=0)
    vals = jnp.concatenate([flat(v3), flat(v2), flat(v1), flat(v0)], axis=0)
    ones = jnp.ones((WIN * rows, HEAD), jnp.bfloat16)
    vaug = jnp.concatenate([vals, ones], axis=1)
    for h in range(heads):
        cols = slice(h * HEAD, (h + 1) * HEAD)
        band = slice(h * rows, (h + 1) * rows)
        qh = q_ref[0, 0, :, cols]
        gh = g_ref[0, 0, :, cols]
        s = lax.dot_general(qh, keys, NT, preferred_element_type=jnp.float32) + bias_ref[...]
        m = jnp.max(s, axis=1, keepdims=True)
        p = jnp.exp2((s - m) * c2)
        pb = p.astype(jnp.bfloat16)
        p_all[band, :] = pb
        o = jnp.dot(pb, vaug, preferred_element_type=jnp.float32)
        inv = 1.0 / o[:, HEAD:]
        att = (o[:, :HEAD] * inv).astype(jnp.bfloat16)
        att_ref[0, 0, :, cols] = att
        g32 = gh.astype(jnp.float32)
        delta = jnp.sum(g32 * att.astype(jnp.float32), axis=1, keepdims=True)
        dp = lax.dot_general(gh, vals, NT, preferred_element_type=jnp.float32)
        ds = (p * (dp - delta)).astype(jnp.bfloat16)
        ds_all[band, :] = ds
        invs = inv * scale
        gs_all[band, :] = (g32 * inv).astype(jnp.bfloat16)
        qs_all[band, :] = (qh.astype(jnp.float32) * invs).astype(jnp.bfloat16)
        dq = jnp.dot(ds, keys, preferred_element_type=jnp.float32) * invs
        dq_ref[0, 0, :, cols] = dq.astype(jnp.bfloat16)
    dk = lax.dot_general(ds_all[...], qs_all[...], TN, preferred_element_type=jnp.float32)
    dv = lax.dot_general(p_all[...], gs_all[...], TN, preferred_element_type=jnp.float32)
    split = (WIN - 1) * rows
    far_ref[0] = dk[:split].astype(jnp.bfloat16).reshape(far_ref.shape[1:])
    far_ref[1] = dv[:split].astype(jnp.bfloat16).reshape(far_ref.shape[1:])
    near_ref[0] = dk[split:]
    near_ref[1] = dv[split:]


def attend(edge, info, lens, reach, queries, grads, blocks, att=None, dq=None):
    rows = queries.shape[2]
    width = queries.shape[3]
    kvw = blocks[0][0].shape[-1]
    steps = kvw // HEAD
    group = width // kvw * HEAD
    slot = lambda info: info[edge]
    wide = pl.BlockSpec((1, 1, rows, group), lambda j, info, *_: (0, slot(info), 0, j))
    in_specs = [wide, wide]
    operands = [queries, grads]
    for array, index in blocks:
        for half in (0, 1):
            if index is None:
                pick = lambda j, info, *_, half=half: (half, slot(info), 0, j)
            else:
                pick = lambda j, info, *_, half=half, index=index: (half, index, 0, j)
            in_specs.append(pl.BlockSpec((1, 1, rows, HEAD), pick))
            operands.append(array)
    aliases = {}
    if att is not None:
        aliases = {3 + len(operands): 0, 4 + len(operands): 1}
        in_specs += [pl.BlockSpec(memory_space=pl.ANY)] * 2
        operands += [att, dq]
    bf = jnp.bfloat16
    out_shape = (
        jax.ShapeDtypeStruct(queries.shape, bf),
        jax.ShapeDtypeStruct(queries.shape, bf),
        jax.ShapeDtypeStruct((2, WIN - 1, rows, kvw), bf),
        jax.ShapeDtypeStruct((2, rows, kvw), jnp.float32),
    )
    out_specs = (
        wide,
        wide,
        pl.BlockSpec((2, WIN - 1, rows, HEAD), lambda j, *_: (0, 0, 0, j)),
        pl.BlockSpec((2, rows, HEAD), lambda j, *_: (0, 0, j)),
    )
    heads = group // HEAD
    tall = heads * rows
    kernel = lambda *refs: attend_kernel(edge, att is not None, *refs)
    return pl.pallas_call(
        kernel,
        out_shape=out_shape,
        grid_spec=pltpu.PrefetchScalarGridSpec(
            num_scalar_prefetch=3,
            grid=(steps,),
            in_specs=in_specs,
            out_specs=out_specs,
            scratch_shapes=[
                pltpu.VMEM((rows, WIN * rows), jnp.float32),
                pltpu.VMEM((tall, WIN * rows), bf),
                pltpu.VMEM((tall, WIN * rows), bf),
                pltpu.VMEM((tall, HEAD), bf),
                pltpu.VMEM((tall, HEAD), bf),
            ],
        ),
        input_output_aliases=aliases,
        name="attend_edge" if edge else "attend_inner",
    )(info, lens, reach, *operands)


def routes(n):
    chips = n // 2
    swap = [(i, i ^ 1) for i in range(n)]
    step = [(2 * c, 2 * c + 2) for c in range(chips - 1)] + [(n - 2, n - 1)]
    step += [(2 * c + 1, 2 * c - 1) for c in range(1, chips)]
    far = [(2 * c + 1, 2 * c + 4) for c in range(chips - 2)]
    far += [(2 * c, 2 * c - 3) for c in range(2, chips)] + [(n - 1, n - 3), (n - 3, n - 1)]
    return swap, step, far


def back(pairs):
    return [(b, a) for a, b in pairs]


def shards(queries, key_heads, value_heads, out_grad, doc_lengths, block_reach):
    n = lax.axis_size("seq")
    me = lax.axis_index("seq")
    core = me % 2
    odd = core == 1
    swap, step, far = routes(n)
    send = lambda x, pairs: lax.ppermute(x, "seq", pairs)
    f32 = jnp.float32
    low, high = me, 2 * n - 1 - me
    info = jnp.stack([1 - core, core, jnp.where(odd, low, high), jnp.where(odd, high, low)])

    own = jnp.stack([key_heads[0], value_heads[0]])
    sib = send(own, swap)
    pick = lambda x, c: jnp.where(c, x[:, 1], x[:, 0])
    edge_pair = jnp.stack([pick(own, odd), pick(sib, odd)], axis=1)
    sib_inner = pick(sib, ~odd)[:, None]
    third = send(pick(own, ~odd)[:, None], far)
    r1 = send(edge_pair, step)
    r2 = send(r1, swap)

    att, dq, inner_far, inner_near = attend(
        0, info, doc_lengths, block_reach, queries, out_grad,
        [(r2, 0), (r2, 1), (sib_inner, 0), (own, None)])
    got = send(inner_far, swap)
    att, dq, edge_far, edge_near = attend(
        1, info, doc_lengths, block_reach, queries, out_grad,
        [(third, 0), (r1, 0), (r1, 1), (own, None)], att, dq)

    third_back = send(edge_far[:, :1], back(far))
    both = (edge_far[:, 1:].astype(f32) + got[:, :2].astype(f32)).astype(jnp.bfloat16)
    r1_back = send(both, back(step))
    rest = send(r1_back[:, 1:], swap)
    edge_total = edge_near + got[:, 2].astype(f32) + r1_back[:, 0].astype(f32)
    inner_total = inner_near + third_back[:, 0].astype(f32) + rest[:, 0].astype(f32)
    total = jnp.stack([jnp.where(odd, inner_total, edge_total),
                       jnp.where(odd, edge_total, inner_total)], axis=1).astype(jnp.bfloat16)
    return att, dq, total[0][None], total[1][None]


def solution(mesh):
    wide = P(("dp", "seq"), None, None, None)
    return jax.shard_map(
        shards,
        mesh=mesh,
        in_specs=(wide, wide, wide, wide, P("dp"), P("dp")),
        out_specs=(wide, wide, wide, wide),
        check_vma=False,
    )
```

time: 142 us -> 104 us (0.73)
  the two profiles are of different devices: /device:TPU:56 before, /device:TPU:17 now
where the time goes in v1:
time: 104 us; the launch traced here: 103 us
  Pallas kernels  45.5 us (44%)
  waiting for transfers between devices  31.9 us (31%)
  starting transfers between devices  16.6 us (16%)
  local copies, waits for them, and re-layouts  4.76 us (5%)
  other arithmetic  3.86 us (4%)
    pallas_call x2, Pallas kernels, attend(): pl.pallas_call(kernel, out_shape=out_shape, grid_spec=pltpu.PrefetchScala...  45.5 us
    ppermute x8, waiting for transfers between devices, shards(): send = lambda x, pairs: lax.ppermute(x, 'seq', pairs)  31.9 us
    ppermute x8, starting transfers between devices, shards(): send = lambda x, pairs: lax.ppermute(x, 'seq', pairs)  16.6 us
    unnamed x15, local copies, waits for them, and re-layouts  2.49 us
  transfers between devices with their start and end apart: 8, of which 6 were waited for; matrix products, arithmetic and copies ran while one was open for 1% of the time, Pallas kernels for 22%

profile of v1, /device:TPU:17, one launch (start us, length us, event | category | flops | bytes accessed | tf_op | source)
XLA Modules:
  0.0 103.4 jit_solution(8091494278130418544)
XLA Ops:
  0.6 1.0 constant_dynamic-update-slice_fusion.1
  1.6 1.0 constant_dynamic-update-slice_fusion.refs_11_.refs_12_
  2.6 0.0 copy-start
  2.6 0.8 collective-permute-start.1
  3.4 1.5 %collective-permute-done.1 = bf16[2,2,128,512]{3,2,1,0:T(8,128)(2,1)S(1)} collective-permute-done((bf16[2,2,128,512]{3,2,1,0:T(8,128)(2,1)S(1)}, bf16[2,2,128,512]{3,2,1,0:T(8,128)(2,1)S(1)}, u32[]{:S(2)}, u32[]{:S(2)}) %collective-permute-start.1) | collective-permute-done | bytes 524320 | tf_op jit(solution)/shard_map/ppermute | solution.py:169
  4.9 0.7 broadcast_select_fusion.2
  5.6 0.1 pad_maximum_fusion
  5.7 4.3 %collective-permute-start.2 = (bf16[2,2,128,512]{3,2,1,0:T(8,128)(2,1)S(1)}, bf16[2,2,128,512]{3,2,1,0:T(8,128)(2,1)S(1)}, u32[]{:S(2)}, u32[]{:S(2)}) collective-permute-start(bf16[2,2,128,512]{3,2,1,0:T(8,128)(2,1)S(1)} %pad_maximum_fusion), channel_id=1, source_target_pairs={{0,2},{2,4},{4,6},{6,8},{8,10},{10,12},{12,14},{14,16},{16,18},{18... | collective-permute-start | bytes 1572872 | tf_op jit(solution)/shard_map/ppermute | solution.py:169
  10.0 6.1 %collective-permute-done.2.refs_7_.refs_8_.refs_9_.refs_10_ = bf16[2,2,128,512]{3,2,1,0:T(8,128)(2,1)S(1)} collective-permute-done((bf16[2,2,128,512]{3,2,1,0:T(8,128)(2,1)S(1)}, bf16[2,2,128,512]{3,2,1,0:T(8,128)(2,1)S(1)}, u32[]{:S(2)}, u32[]{:S(2)}) %collective-permute-start.2) | collective-permute-done | bytes 524320 | tf_op jit(solution)/shard_map/ppermute | solution.py:169
  16.1 0.0 copy-start.1
  16.1 3.2 %collective-permute-start.3 = (bf16[2,2,128,512]{3,2,1,0:T(8,128)(2,1)S(1)}, bf16[2,2,128,512]{3,2,1,0:T(8,128)(2,1)S(1)}, u32[]{:S(2)}, u32[]{:S(2)}) collective-permute-start(bf16[2,2,128,512]{3,2,1,0:T(8,128)(2,1)S(1)} %collective-permute-done.2.refs_7_.refs_8_.refs_9_.refs_10_), channel_id=1, source_target_pairs={{0,1},{1,0},{2,3},{3,2},{4,5},{5,4},{6,7},{7,6},{8,9},{9,8},{10,11... | collective-permute-start | bytes 1572872 | tf_op jit(solution)/shard_map/ppermute | solution.py:169
  19.2 0.6 pad_add_fusion.refs_0_
  19.9 0.9 collective-permute-done.3.refs_5_.refs_6_.refs_7_.refs_8_
  20.8 0.0 copy-start.2
  20.8 0.0 copy-done
  20.8 0.8 copy-done.2
  21.6 22.7 %attend_inner.1 = (bf16[1,2,128,4096]{3,2,1,0:T(8,128)(2,1)}, bf16[1,2,128,4096]{3,2,1,0:T(8,128)(2,1)}, bf16[2,3,128,512]{3,2,1,0:T(8,128)(2,1)}, f32[2,128,512]{2,1,0:T(8,128)}) custom-call(s32[4]{0:T(128)} %pad_add_fusion.refs_0_, s32[32]{0:T(128)} %refs_1_.3, s32[64]{0:T(128)} %refs_2_.3, bf16[1,2,128,4096]{3,2,1,0:T(8,128)(2,1)} %refs_3_.3, ...), custom_call_target="tpu_custom_call" | custom-call | tf_op jit(solution)/shard_map/attend_inner/pallas_call | solution.py:128
  44.3 0.0 copy-done.1
  44.3 1.2 %copy.14 = bf16[2,3,128,512]{3,2,0,1:T(8,128)(2,1)S(1)} copy(bf16[2,3,128,512]{3,2,1,0:T(8,128)(2,1)} %get-tuple-element.18) | data formatting | bytes 1572864 | tf_op jit(solution)/shard_map/attend_inner/pallas_call | solution.py:128
  45.5 0.5 collective-permute-start.5
  46.1 2.5 %collective-permute-start = (bf16[2,1,128,512]{3,2,1,0:T(8,128)(2,1)S(1)}, bf16[2,1,128,512]{3,2,1,0:T(8,128)(2,1)S(1)}, u32[]{:S(2)}, u32[]{:S(2)}) collective-permute-start(bf16[2,1,128,512]{3,2,1,0:T(8,128)(2,1)S(1)} %get-tuple-element.31), channel_id=1, source_target_pairs={{1,4},{3,6},{5,8},{7,10},{9,12},{11,14},{13,16},{15,18},{17,20},{1... | collective-permute-start | bytes 786440 | tf_op jit(solution)/shard_map/ppermute | solution.py:169
  48.5 9.7 %collective-permute-done.refs_5_.refs_6_ = bf16[2,1,128,512]{3,2,1,0:T(8,128)(2,1)S(1)} collective-permute-done((bf16[2,1,128,512]{3,2,1,0:T(8,128)(2,1)S(1)}, bf16[2,1,128,512]{3,2,1,0:T(8,128)(2,1)S(1)}, u32[]{:S(2)}, u32[]{:S(2)}) %collective-permute-start) | collective-permute-done | bytes 262176 | tf_op jit(solution)/shard_map/ppermute | solution.py:169
  58.2 0.0 copy-start.4
  58.2 0.7 copy-done.4
  58.9 22.8 %attend_edge.1 = (bf16[1,2,128,4096]{3,2,1,0:T(8,128)(2,1)}, bf16[1,2,128,4096]{3,2,1,0:T(8,128)(2,1)}, bf16[2,3,128,512]{3,2,1,0:T(8,128)(2,1)}, f32[2,128,512]{2,1,0:T(8,128)}) custom-call(s32[4]{0:T(128)} %pad_add_fusion.refs_0_, s32[32]{0:T(128)} %refs_1_.3, s32[64]{0:T(128)} %refs_2_.3, ...), custom_call_target="tpu_custom_call", output_to_operand_aliasing={{0}: (13, {}), {1}: (14, {})} | custom-call | tf_op jit(solution)/shard_map/attend_edge/pallas_call | solution.py:128
  81.7 0.0 copy-start.3
  81.7 0.0 collective-permute-done.5
  81.7 0.0 copy-start.5
  81.7 0.0 copy-start.6
  81.8 1.3 %add_convert_fusion = bf16[2,2,128,512]{3,2,0,1:T(8,128)(2,1)S(1)} fusion(bf16[2,3,128,512]{3,2,0,1:T(8,128)(2,1)S(1)} %collective-permute-done.5, bf16[2,3,128,512]{3,2,1,0:T(8,128)(2,1)} %get-tuple-element.17), kind=kLoop, calls=%fused_computation | loop fusion | flops 1048576 | bytes 1572864 | tf_op jit(solution)/shard_map/convert_element_type | solution.py:192
  83.1 1.9 %collective-permute-start.6 = (bf16[2,2,128,512]{3,2,0,1:T(8,128)(2,1)S(1)}, bf16[2,2,128,512]{3,2,0,1:T(8,128)(2,1)S(1)}, u32[]{:S(2)}, u32[]{:S(2)}) collective-permute-start(bf16[2,2,128,512]{3,2,0,1:T(8,128)(2,1)S(1)} %add_convert_fusion), channel_id=1, source_target_pairs={{2,0},{4,2},{6,4},{8,6},{10,8},{12,10},{14,12},{16,14},{18,16},{20... | collective-permute-start | bytes 1572872 | tf_op jit(solution)/shard_map/ppermute | solution.py:169
  85.0 0.0 copy-done.3
  85.0 0.1 copy.12
  85.1 3.3 %collective-permute-start.4 = (bf16[2,1,128,512]{3,2,0,1:T(8,128)(2,1)S(1)}, bf16[2,1,128,512]{3,2,0,1:T(8,128)(2,1)S(1)}, u32[]{:S(2)}, u32[]{:S(2)}) collective-permute-start(bf16[2,1,128,512]{3,2,0,1:T(8,128)(2,1)S(1)} %slice.56), channel_id=1, source_target_pairs={{4,1},{6,3},{8,5},{10,7},{12,9},{14,11},{16,13},{18,15},{20,17},{2... | collective-permute-start | bytes 786440 | tf_op jit(solution)/shard_map/ppermute | solution.py:169
  88.5 12.2 %collective-permute-done.6 = bf16[2,2,128,512]{3,2,0,1:T(8,128)(2,1)S(1)} collective-permute-done((bf16[2,2,128,512]{3,2,0,1:T(8,128)(2,1)S(1)}, bf16[2,2,128,512]{3,2,0,1:T(8,128)(2,1)S(1)}, u32[]{:S(2)}, u32[]{:S(2)}) %collective-permute-start.6) | collective-permute-done | bytes 524320 | tf_op jit(solution)/shard_map/ppermute | solution.py:169
  100.7 0.1 collective-permute-start.7
  100.8 0.0 collective-permute-done.4
  100.8 1.5 %collective-permute-done.7 = bf16[2,1,128,512]{3,2,0,1:T(8,128)(2,1)S(1)} collective-permute-done((bf16[2,1,128,512]{3,2,0,1:T(8,128)(2,1)S(1)}, bf16[2,1,128,512]{3,2,0,1:T(8,128)(2,1)S(1)}, u32[]{:S(2)}, u32[]{:S(2)}) %collective-permute-start.7) | collective-permute-done | bytes 262176 | tf_op jit(solution)/shard_map/ppermute | solution.py:169
  102.4 0.0 copy-done.5
  102.4 0.0 copy-done.6
  102.4 0.2 fusion.1
  102.6 0.8 fusion.4
  (3 shorter events, 0.1 us)
Async XLA Ops:
  2.6 18.2 %copy-start = (bf16[2,2,128,512]{3,2,1,0:T(8,128)(2,1)}, bf16[2,2,128,512]{3,2,1,0:T(8,128)(2,1)S(1)}, u32[]{:S(2)}) copy-start(bf16[2,2,128,512]{3,2,1,0:T(8,128)(2,1)S(1)} %constant_dynamic-update-slice_fusion.refs_11_.refs_12_) | copy-start | bytes 1572868
  2.6 2.3 %collective-permute-start.1 = (bf16[2,2,128,512]{3,2,1,0:T(8,128)(2,1)S(1)}, bf16[2,2,128,512]{3,2,1,0:T(8,128)(2,1)S(1)}, u32[]{:S(2)}, u32[]{:S(2)}) collective-permute-start(bf16[2,2,128,512]{3,2,1,0:T(8,128)(2,1)S(1)} %constant_dynamic-update-slice_fusion.refs_11_.refs_12_), channel_id=1, source_target_pairs={{0,1},{1,0},{2,3},{3,2},{4,5},{5,4},{6,7},{7,6},{8,9},{9,8},{10,11... | collective-permute-start | bytes 1572872 | tf_op jit(solution)/shard_map/ppermute | solution.py:169
  5.7 10.4 %collective-permute-start.2 = (bf16[2,2,128,512]{3,2,1,0:T(8,128)(2,1)S(1)}, bf16[2,2,128,512]{3,2,1,0:T(8,128)(2,1)S(1)}, u32[]{:S(2)}, u32[]{:S(2)}) collective-permute-start(bf16[2,2,128,512]{3,2,1,0:T(8,128)(2,1)S(1)} %pad_maximum_fusion), channel_id=1, source_target_pairs={{0,2},{2,4},{4,6},{6,8},{8,10},{10,12},{12,14},{14,16},{16,18},{18... | collective-permute-start | bytes 1572872 | tf_op jit(solution)/shard_map/ppermute | solution.py:169
  16.1 28.3 %copy-start.1 = (bf16[2,2,128,512]{3,2,1,0:T(8,128)(2,1)}, bf16[2,2,128,512]{3,2,1,0:T(8,128)(2,1)S(1)}, u32[]{:S(2)}) copy-start(bf16[2,2,128,512]{3,2,1,0:T(8,128)(2,1)S(1)} %collective-permute-done.2.refs_7_.refs_8_.refs_9_.refs_10_) | copy-start | bytes 1572868
  16.1 4.7 %collective-permute-start.3 = (bf16[2,2,128,512]{3,2,1,0:T(8,128)(2,1)S(1)}, bf16[2,2,128,512]{3,2,1,0:T(8,128)(2,1)S(1)}, u32[]{:S(2)}, u32[]{:S(2)}) collective-permute-start(bf16[2,2,128,512]{3,2,1,0:T(8,128)(2,1)S(1)} %collective-permute-done.2.refs_7_.refs_8_.refs_9_.refs_10_), channel_id=1, source_target_pairs={{0,1},{1,0},{2,3},{3,2},{4,5},{5,4},{6,7},{7,6},{8,9},{9,8},{10,11... | collective-permute-start | bytes 1572872 | tf_op jit(solution)/shard_map/ppermute | solution.py:169
  20.8 0.8 copy-start.2
  45.5 36.2 %collective-permute-start.5 = (bf16[2,3,128,512]{3,2,0,1:T(8,128)(2,1)S(1)}, bf16[2,3,128,512]{3,2,0,1:T(8,128)(2,1)S(1)}, u32[]{:S(2)}, u32[]{:S(2)}) collective-permute-start(bf16[2,3,128,512]{3,2,0,1:T(8,128)(2,1)S(1)} %copy.14), channel_id=1, source_target_pairs={{0,1},{1,0},{2,3},{3,2},{4,5},{5,4},{6,7},{7,6},{8,9},{9,8},{10,11... | collective-permute-start | bytes 2359304 | tf_op jit(solution)/shard_map/ppermute | solution.py:169
  46.1 12.2 %collective-permute-start = (bf16[2,1,128,512]{3,2,1,0:T(8,128)(2,1)S(1)}, bf16[2,1,128,512]{3,2,1,0:T(8,128)(2,1)S(1)}, u32[]{:S(2)}, u32[]{:S(2)}) collective-permute-start(bf16[2,1,128,512]{3,2,1,0:T(8,128)(2,1)S(1)} %get-tuple-element.31), channel_id=1, source_target_pairs={{1,4},{3,6},{5,8},{7,10},{9,12},{11,14},{13,16},{15,18},{17,20},{1... | collective-permute-start | bytes 786440 | tf_op jit(solution)/shard_map/ppermute | solution.py:169
  58.2 0.7 copy-start.4
  81.7 3.3 %copy-start.3 = (bf16[2,3,128,512]{3,2,1,0:T(8,128)(2,1)S(1)}, bf16[2,3,128,512]{3,2,1,0:T(8,128)(2,1)}, u32[]{:S(2)}) copy-start(bf16[2,3,128,512]{3,2,1,0:T(8,128)(2,1)} %get-tuple-element.17) | copy-start | bytes 2359300
  81.7 20.6 %copy-start.5 = (f32[2,128,512]{2,1,0:T(8,128)S(1)}, f32[2,128,512]{2,1,0:T(8,128)}, u32[]{:S(2)}) copy-start(f32[2,128,512]{2,1,0:T(8,128)} %get-tuple-element.16) | copy-start | bytes 1572868
  81.7 20.6 %copy-start.6 = (f32[2,128,512]{2,1,0:T(8,128)S(1)}, f32[2,128,512]{2,1,0:T(8,128)}, u32[]{:S(2)}) copy-start(f32[2,128,512]{2,1,0:T(8,128)} %get-tuple-element.19) | copy-start | bytes 1572868
  83.1 17.7 %collective-permute-start.6 = (bf16[2,2,128,512]{3,2,0,1:T(8,128)(2,1)S(1)}, bf16[2,2,128,512]{3,2,0,1:T(8,128)(2,1)S(1)}, u32[]{:S(2)}, u32[]{:S(2)}) collective-permute-start(bf16[2,2,128,512]{3,2,0,1:T(8,128)(2,1)S(1)} %add_convert_fusion), channel_id=1, source_target_pairs={{2,0},{4,2},{6,4},{8,6},{10,8},{12,10},{14,12},{16,14},{18,16},{20... | collective-permute-start | bytes 1572872 | tf_op jit(solution)/shard_map/ppermute | solution.py:169
  85.1 15.7 %collective-permute-start.4 = (bf16[2,1,128,512]{3,2,0,1:T(8,128)(2,1)S(1)}, bf16[2,1,128,512]{3,2,0,1:T(8,128)(2,1)S(1)}, u32[]{:S(2)}, u32[]{:S(2)}) collective-permute-start(bf16[2,1,128,512]{3,2,0,1:T(8,128)(2,1)S(1)} %slice.56), channel_id=1, source_target_pairs={{4,1},{6,3},{8,5},{10,7},{12,9},{14,11},{16,13},{18,15},{20,17},{2... | collective-permute-start | bytes 786440 | tf_op jit(solution)/shard_map/ppermute | solution.py:169
  100.7 1.6 %collective-permute-start.7 = (bf16[2,1,128,512]{3,2,0,1:T(8,128)(2,1)S(1)}, bf16[2,1,128,512]{3,2,0,1:T(8,128)(2,1)S(1)}, u32[]{:S(2)}, u32[]{:S(2)}) collective-permute-start(bf16[2,1,128,512]{3,2,0,1:T(8,128)(2,1)S(1)} %slice.59), channel_id=1, source_target_pairs={{0,1},{1,0},{2,3},{3,2},{4,5},{5,4},{6,7},{7,6},{8,9},{9,8},{10,11... | collective-permute-start | bytes 786440 | tf_op jit(solution)/shard_map/ppermute | solution.py:169
